TPU v7x, 32 devices: a whole 2x2x4 slice. The times are simulated.
32 devices in a mesh: ctx: 8 (over z, x), head: 4 (over y, core).
Axes of the slice: x: 2, y: 2, z: 4, core: 2. Of those that a mesh axis runs over, the one named last changes fastest.
Arguments:
- queries: bfloat16 [8192, 512], P('ctx', 'head'), may hold values from -6 to 6
- keys: bfloat16 [8192, 512], P('ctx', 'head'), may hold values from -6 to 6
- values: bfloat16 [8192, 512], P('ctx', 'head'), may hold values from -6 to 6
- write_rates: float32 [4, 8192], P('head', 'ctx'), may hold values from 0 to 2, as said below
- norm_gain: float32 [128], replicated, may hold values from 0.1 to 1.9
- w_out: bfloat16 [512, 2048], P(None, 'head'), may hold values from -0.25 to 0.25
Outputs:
- mixed: bfloat16 [8192, 2048], P('ctx', 'head')
Inputs may be any that keep to these rules, and one draw needn't show every extreme that they name: `write_rates`: every rate lies strictly between 0 and 2.
All inputs are finite; a program needn't handle non-finite values.
Results may differ from a plain program's by a relative error of at most 0.0049.
Values may be sent and summed in bfloat16 or wider, within the bound.
A program may use at most 64 MiB of HBM per device.

v0:
```python
import jax
import jax.numpy as jnp
from jax import lax
from jax.sharding import PartitionSpec as P

HEAD_DIM = 128
GROUP = 128


def passed_along(value, axis, steps):
    count = lax.axis_size(axis)
    leading, last = (max(0, -steps), min(count, count - steps))
    return lax.ppermute(value, axis, [(source, source + steps) for source in range(leading, last)])


def matmul(left, right):
    return jnp.dot(left, right, precision=lax.Precision.HIGHEST, preferred_element_type=jnp.float32)


def unit_rows(matrix):
    wide = matrix.astype(jnp.float32)
    return wide / jnp.sqrt(jnp.sum(wide * wide, axis=-1, keepdims=True) + 1e-06)


def block_parts(query_block, key_block, value_block, rate_block):
    width = key_block.shape[1]
    gram = matmul(key_block, key_block.T)
    lower = jnp.tril(rate_block[:, None] * gram, -1) + jnp.eye(
        key_block.shape[0], dtype=jnp.float32
    )
    stacked = jnp.concatenate(
        [rate_block[:, None] * key_block, rate_block[:, None] * value_block], axis=1
    )
    solved = jax.scipy.linalg.solve_triangular(lower, stacked, lower=True, unit_diagonal=True)
    wy_keys = solved[:, :width]
    wy_values = solved[:, width:]
    transition = jnp.eye(width, dtype=jnp.float32) - matmul(wy_keys.T, key_block)
    offset = matmul(wy_values.T, key_block)
    scores = jnp.tril(matmul(query_block, key_block.T))
    return (wy_keys, wy_values, transition, offset, scores)


def block_output(state, query_block, wy_keys, wy_values, transition, offset, scores):
    result = matmul(query_block, state.T) + matmul(scores, wy_values - matmul(wy_keys, state.T))
    return (result, matmul(state, transition) + offset)


def shards(queries, keys, values, write_rates, norm_gain, w_out):
    length = queries.shape[0]
    blocks = length // GROUP
    query_rows = unit_rows(queries).reshape(blocks, GROUP, HEAD_DIM)
    key_rows = unit_rows(keys).reshape(blocks, GROUP, HEAD_DIM)
    value_rows = values.astype(jnp.float32).reshape(blocks, GROUP, HEAD_DIM)
    rate_rows = write_rates[0].reshape(blocks, GROUP)
    wy_keys, wy_values, transition, offset, scores = jax.vmap(block_parts)(
        query_rows, key_rows, value_rows, rate_rows
    )
    identity_hd = jnp.eye(HEAD_DIM, dtype=jnp.float32)
    zero_state = jnp.zeros((HEAD_DIM, HEAD_DIM), jnp.float32)

    def compose(carry, step):
        return ((matmul(carry[0], step[0]), matmul(carry[1], step[0]) + step[1]), None)

    (device_map, device_offset), unused = lax.scan(
        compose, (identity_hd, zero_state), (transition, offset)
    )

    def relay(step, state):
        return passed_along(matmul(state, device_map) + device_offset, "ctx", 1)

    start_state = lax.fori_loop(0, lax.axis_size("ctx") - 1, relay, zero_state)

    def advance(state, block):
        result, state = block_output(state, *block)
        return (state, result)

    final, outputs = lax.scan(
        advance, start_state, (query_rows, wy_keys, wy_values, transition, offset, scores)
    )
    outputs = outputs.reshape(length, HEAD_DIM)
    normed = (
        outputs * lax.rsqrt(jnp.mean(outputs * outputs, axis=-1, keepdims=True) + 1e-06) * norm_gain
    ).astype(jnp.bfloat16)
    token_rows = lax.all_to_all(normed, "head", split_axis=0, concat_axis=1, tiled=True)
    full_rows = jnp.dot(
        token_rows,
        lax.all_gather(w_out, "head", axis=1, tiled=True),
        preferred_element_type=jnp.float32,
    ).astype(jnp.bfloat16)
    return lax.all_to_all(full_rows, "head", split_axis=1, concat_axis=0, tiled=True)


def solution(mesh):
    return jax.shard_map(
        shards,
        mesh=mesh,
        in_specs=(
            P("ctx", "head"),
            P("ctx", "head"),
            P("ctx", "head"),
            P("head", "ctx"),
            P(),
            P(None, "head"),
        ),
        out_specs=P("ctx", "head"),
        check_vma=False,
    )
```

profile of v0, /device:TPU:24, one launch (start us, length us, event | category | flops | bytes accessed | tf_op | source)
XLA Modules:
  0.0 204.3 jit_solution(2503386418949848491)
XLA Ops:
  6.5 0.7 all-gather.2.cloned.1.call-update
  7.3 1.2 fusion.36
  8.5 1.2 convert_divide_fusion.1
  9.8 1.9 fusion.31
  11.8 78.6 %custom-call.4 = f32[8,1,128,128]{2,3,1,0:T(8,128)S(1)} custom-call(f32[8,1,128,128]{3,2,1,0:T(8,128)S(1)} %fusion.31), custom_call_target="InvertDiagBlocksLowerTriangular" | custom-call | tf_op jit(solution)/shard_map/vmap(jit(_solve_triangular))/triangular_solve | solution.py:34
  90.4 0.2 broadcast_multiply_fusion
  90.6 1.0 fusion.32
  91.6 1.0 convolution_subtract_fusion.1
  92.7 1.0 fusion.44
  93.7 1.1 fusion.47
  94.8 5.2 %while.40 = (s32[]{:T(128)}, f32[128,128]{0,1:T(8,128)S(1)}, f32[128,128]{0,1:T(8,128)S(1)}, f32[8,128,128]{2,1,0:T(8,128)S(1)}, f32[8,128,128]{1,2,0:T(8,128)S(1)}) while((s32[]{:T(128)}, f32[128,128]{0,1:T(8,128)S(1)}, f32[128,128]{0,1:T(8,128)S(1)}, f32[8,128,128]{2,1,0:T(8,128)S(1)}, ...), condition=%wide.region_2.3_spmd.clone.clone, body=%wide.region_1.0_spmd.clone.sunk.clone | while | flops 50364416 | bytes 721995 | solution.py:64
  94.8 0.3 fusion.116
  95.1 0.3 convolution_bitcast_fusion.5
  95.5 0.3 fusion.116
  95.8 0.3 convolution_bitcast_fusion.5
  96.1 0.3 fusion.116
  96.4 0.3 convolution_bitcast_fusion.5
  96.8 0.3 fusion.116
  97.1 0.3 convolution_bitcast_fusion.5
  97.4 0.3 fusion.116
  97.7 0.3 convolution_bitcast_fusion.5
  98.1 0.3 fusion.116
  98.4 0.3 convolution_bitcast_fusion.5
  98.7 0.3 fusion.116
  99.0 0.3 convolution_bitcast_fusion.5
  99.4 0.3 fusion.116
  99.7 0.3 convolution_bitcast_fusion.5
  100.2 51.2 %while.38 = (s32[]{:T(128)}, f32[128,128]{1,0:T(8,128)S(1)}, f32[128,128]{1,0:T(8,128)S(1)}, f32[128,128]{1,0:T(8,128)S(1)}) while((s32[]{:T(128)}, f32[128,128]{1,0:T(8,128)S(1)}, f32[128,128]{1,0:T(8,128)S(1)}, f32[128,128]{1,0:T(8,128)S(1)}) %tuple.75), condition=%wide.region_4.5_spmd.clone, body=%wide.region_3.4_spmd.sunk.clone | while | flops 25182208 | bytes 524381 | solution.py:71
  100.4 3.4 %collective-permute-start = (f32[128,128]{1,0:T(8,128)S(1)}, f32[128,128]{1,0:T(8,128)S(1)}, u32[]{:S(2)}, u32[]{:S(2)}) collective-permute-start(f32[128,128]{1,0:T(8,128)S(1)} %convolution_add_fusion.4), channel_id=1, source_target_pairs={{0,4},{4,8},{8,12},{12,16},{16,20},{20,24},{24,28},{1,5},{5,9},{9,... | collective-permute-start | bytes 196616 | tf_op jit(solution)/shard_map/while/body/eval_jaxpr/ppermute | solution.py:13
  103.8 3.6 %collective-permute-done = f32[128,128]{1,0:T(8,128)S(1)} collective-permute-done((f32[128,128]{1,0:T(8,128)S(1)}, f32[128,128]{1,0:T(8,128)S(1)}, u32[]{:S(2)}, u32[]{:S(2)}) %collective-permute-start) | collective-permute-done | bytes 65568 | tf_op jit(solution)/shard_map/while/body/eval_jaxpr/ppermute | solution.py:13
  107.7 2.5 %collective-permute-start = (f32[128,128]{1,0:T(8,128)S(1)}, f32[128,128]{1,0:T(8,128)S(1)}, u32[]{:S(2)}, u32[]{:S(2)}) collective-permute-start(f32[128,128]{1,0:T(8,128)S(1)} %convolution_add_fusion.4), channel_id=1, source_target_pairs={{0,4},{4,8},{8,12},{12,16},{16,20},{20,24},{24,28},{1,5},{5,9},{9,... | collective-permute-start | bytes 196616 | tf_op jit(solution)/shard_map/while/body/eval_jaxpr/ppermute | solution.py:13
  110.2 4.5 %collective-permute-done = f32[128,128]{1,0:T(8,128)S(1)} collective-permute-done((f32[128,128]{1,0:T(8,128)S(1)}, f32[128,128]{1,0:T(8,128)S(1)}, u32[]{:S(2)}, u32[]{:S(2)}) %collective-permute-start) | collective-permute-done | bytes 65568 | tf_op jit(solution)/shard_map/while/body/eval_jaxpr/ppermute | solution.py:13
  115.0 1.9 collective-permute-start
  116.9 5.1 %collective-permute-done = f32[128,128]{1,0:T(8,128)S(1)} collective-permute-done((f32[128,128]{1,0:T(8,128)S(1)}, f32[128,128]{1,0:T(8,128)S(1)}, u32[]{:S(2)}, u32[]{:S(2)}) %collective-permute-start) | collective-permute-done | bytes 65568 | tf_op jit(solution)/shard_map/while/body/eval_jaxpr/ppermute | solution.py:13
  122.2 1.9 collective-permute-start
  124.2 5.1 %collective-permute-done = f32[128,128]{1,0:T(8,128)S(1)} collective-permute-done((f32[128,128]{1,0:T(8,128)S(1)}, f32[128,128]{1,0:T(8,128)S(1)}, u32[]{:S(2)}, u32[]{:S(2)}) %collective-permute-start) | collective-permute-done | bytes 65568 | tf_op jit(solution)/shard_map/while/body/eval_jaxpr/ppermute | solution.py:13
  129.5 1.9 collective-permute-start
  131.4 5.4 %collective-permute-done = f32[128,128]{1,0:T(8,128)S(1)} collective-permute-done((f32[128,128]{1,0:T(8,128)S(1)}, f32[128,128]{1,0:T(8,128)S(1)}, u32[]{:S(2)}, u32[]{:S(2)}) %collective-permute-start) | collective-permute-done | bytes 65568 | tf_op jit(solution)/shard_map/while/body/eval_jaxpr/ppermute | solution.py:13
  137.1 1.9 collective-permute-start
  139.0 5.1 %collective-permute-done = f32[128,128]{1,0:T(8,128)S(1)} collective-permute-done((f32[128,128]{1,0:T(8,128)S(1)}, f32[128,128]{1,0:T(8,128)S(1)}, u32[]{:S(2)}, u32[]{:S(2)}) %collective-permute-start) | collective-permute-done | bytes 65568 | tf_op jit(solution)/shard_map/while/body/eval_jaxpr/ppermute | solution.py:13
  144.3 1.9 collective-permute-start
  146.3 5.1 %collective-permute-done = f32[128,128]{1,0:T(8,128)S(1)} collective-permute-done((f32[128,128]{1,0:T(8,128)S(1)}, f32[128,128]{1,0:T(8,128)S(1)}, u32[]{:S(2)}, u32[]{:S(2)}) %collective-permute-start) | collective-permute-done | bytes 65568 | tf_op jit(solution)/shard_map/while/body/eval_jaxpr/ppermute | solution.py:13
  152.0 1.2 convolution_select_fusion
  153.2 14.8 %while.39 = (s32[]{:T(128)}, f32[128,128]{0,1:T(8,128)S(1)}, f32[8,128,128]{2,1,0:T(8,128)S(1)}, f32[8,128,128]{2,1,0:T(8,128)S(1)}, f32[8,128,128]{1,2,0:T(8,12...) while((s32[]{:T(128)}, f32[128,128]{0,1:T(8,128)S(1)}, ...), condition=%wide.region_7.8_spmd.clone, body=%wide.region_6.7_spmd.sunk.clone | while | flops 100712448 | bytes 1117281 | solution.py:77
  153.2 1.1 convolution_subtract_fusion.4
  154.7 0.3 fusion.109
  155.1 1.1 convolution_subtract_fusion.4
  156.6 0.3 fusion.109
  156.9 1.1 convolution_subtract_fusion.4
  158.4 0.3 fusion.109
  158.8 1.1 convolution_subtract_fusion.4
  160.3 0.3 fusion.109
  160.6 1.1 convolution_subtract_fusion.4
  162.1 0.3 fusion.109
  162.4 1.1 convolution_subtract_fusion.4
  164.0 0.3 fusion.109
  164.3 1.1 convolution_subtract_fusion.4
  165.8 0.3 fusion.109
  166.1 1.1 convolution_subtract_fusion.4
  167.7 0.3 fusion.109
  168.4 8.6 %all_to_all.35 = bf16[4,256,128]{2,1,0:T(8,128)(2,1)S(1)} all-to-all(bf16[4,256,128]{2,1,0:T(8,128)(2,1)S(1)} %fusion.39), channel_id=1, replica_groups=mesh['ctx'=8,'head'=4] {'head'}, dimensions={0} | all-to-all | bytes 524288 | tf_op jit(solution)/shard_map/all_to_all | solution.py:84
  177.2 2.3 %convolution_convert_fusion = bf16[256,2048]{1,0:T(8,128)(2,1)S(1)} fusion(bf16[256,512]{0,1:T(8,128)(2,1)S(1)} %bitcast.150, bf16[512,2048]{1,0:T(8,128)(2,1)} %all-gather.2.cloned.1.call-done), kind=kOutput, calls=%fused_computation.33 | convolution fusion | flops 537395200 | bytes 3407872 | tf_op jit(solution)/shard_map/dot_general | solution.py:85
  179.6 16.9 %all_to_all.36 = bf16[256,4,512]{2,0,1:T(8,128)(2,1)S(1)} all-to-all(bf16[256,4,512]{2,0,1:T(8,128)(2,1)S(1)} %bitcast.144), channel_id=1, replica_groups=mesh['ctx'=8,'head'=4] {'head'}, dimensions={1} | all-to-all | bytes 2097152 | tf_op jit(solution)/shard_map/all_to_all | solution.py:90
  196.5 1.0 copy.90
  (78 shorter events, 6.5 us)
Async XLA Ops:
  6.5 83.8 %copy-start.2 = (f32[1,1024]{1,0:T(1,128)S(1)}, f32[1,1024]{1,0:T(1,128)}, u32[]{:S(2)}) copy-start(f32[1,1024]{1,0:T(1,128)} %param.15) | copy-start | bytes 12292
  6.5 83.8 %copy-start.1 = (bf16[1024,128]{1,0:T(8,128)(2,1)S(1)}, bf16[1024,128]{1,0:T(8,128)(2,1)}, u32[]{:S(2)}) copy-start(bf16[1024,128]{1,0:T(8,128)(2,1)} %param.14) | copy-start | bytes 786436
  6.5 170.7 %all-gather.2.cloned.1.call-start = ((), (), s32[]{:S(2)}) async-start(), calls=%async_computation.2 | async-start | bytes 2621440 | tf_op jit(solution)/shard_map/all_gather | solution.py:87
  94.8 56.7 %copy-start = (bf16[1024,128]{1,0:T(8,128)(2,1)S(1)}, bf16[1024,128]{1,0:T(8,128)(2,1)}, u32[]{:S(2)}) copy-start(bf16[1024,128]{1,0:T(8,128)(2,1)} %param.12) | copy-start | bytes 786436
  100.4 7.1 %collective-permute-start = (f32[128,128]{1,0:T(8,128)S(1)}, f32[128,128]{1,0:T(8,128)S(1)}, u32[]{:S(2)}, u32[]{:S(2)}) collective-permute-start(f32[128,128]{1,0:T(8,128)S(1)} %convolution_add_fusion.4), channel_id=1, source_target_pairs={{0,4},{4,8},{8,12},{12,16},{16,20},{20,24},{24,28},{1,5},{5,9},{9,... | collective-permute-start | bytes 196616 | tf_op jit(solution)/shard_map/while/body/eval_jaxpr/ppermute | solution.py:13
  107.7 7.1 %collective-permute-start = (f32[128,128]{1,0:T(8,128)S(1)}, f32[128,128]{1,0:T(8,128)S(1)}, u32[]{:S(2)}, u32[]{:S(2)}) collective-permute-start(f32[128,128]{1,0:T(8,128)S(1)} %convolution_add_fusion.4), channel_id=1, source_target_pairs={{0,4},{4,8},{8,12},{12,16},{16,20},{20,24},{24,28},{1,5},{5,9},{9,... | collective-permute-start | bytes 196616 | tf_op jit(solution)/shard_map/while/body/eval_jaxpr/ppermute | solution.py:13
  115.0 7.1 %collective-permute-start = (f32[128,128]{1,0:T(8,128)S(1)}, f32[128,128]{1,0:T(8,128)S(1)}, u32[]{:S(2)}, u32[]{:S(2)}) collective-permute-start(f32[128,128]{1,0:T(8,128)S(1)} %convolution_add_fusion.4), channel_id=1, source_target_pairs={{0,4},{4,8},{8,12},{12,16},{16,20},{20,24},{24,28},{1,5},{5,9},{9,... | collective-permute-start | bytes 196616 | tf_op jit(solution)/shard_map/while/body/eval_jaxpr/ppermute | solution.py:13
  122.2 7.1 %collective-permute-start = (f32[128,128]{1,0:T(8,128)S(1)}, f32[128,128]{1,0:T(8,128)S(1)}, u32[]{:S(2)}, u32[]{:S(2)}) collective-permute-start(f32[128,128]{1,0:T(8,128)S(1)} %convolution_add_fusion.4), channel_id=1, source_target_pairs={{0,4},{4,8},{8,12},{12,16},{16,20},{20,24},{24,28},{1,5},{5,9},{9,... | collective-permute-start | bytes 196616 | tf_op jit(solution)/shard_map/while/body/eval_jaxpr/ppermute | solution.py:13
  129.5 7.4 %collective-permute-start = (f32[128,128]{1,0:T(8,128)S(1)}, f32[128,128]{1,0:T(8,128)S(1)}, u32[]{:S(2)}, u32[]{:S(2)}) collective-permute-start(f32[128,128]{1,0:T(8,128)S(1)} %convolution_add_fusion.4), channel_id=1, source_target_pairs={{0,4},{4,8},{8,12},{12,16},{16,20},{20,24},{24,28},{1,5},{5,9},{9,... | collective-permute-start | bytes 196616 | tf_op jit(solution)/shard_map/while/body/eval_jaxpr/ppermute | solution.py:13
  137.1 7.1 %collective-permute-start = (f32[128,128]{1,0:T(8,128)S(1)}, f32[128,128]{1,0:T(8,128)S(1)}, u32[]{:S(2)}, u32[]{:S(2)}) collective-permute-start(f32[128,128]{1,0:T(8,128)S(1)} %convolution_add_fusion.4), channel_id=1, source_target_pairs={{0,4},{4,8},{8,12},{12,16},{16,20},{20,24},{24,28},{1,5},{5,9},{9,... | collective-permute-start | bytes 196616 | tf_op jit(solution)/shard_map/while/body/eval_jaxpr/ppermute | solution.py:13
  144.3 7.1 %collective-permute-start = (f32[128,128]{1,0:T(8,128)S(1)}, f32[128,128]{1,0:T(8,128)S(1)}, u32[]{:S(2)}, u32[]{:S(2)}) collective-permute-start(f32[128,128]{1,0:T(8,128)S(1)} %convolution_add_fusion.4), channel_id=1, source_target_pairs={{0,4},{4,8},{8,12},{12,16},{16,20},{20,24},{24,28},{1,5},{5,9},{9,... | collective-permute-start | bytes 196616 | tf_op jit(solution)/shard_map/while/body/eval_jaxpr/ppermute | solution.py:13
  153.2 15.0 %copy-start.3 = (f32[128]{0:T(128)S(1)}, f32[128]{0:T(128)}, u32[]{:S(2)}) copy-start(f32[128]{0:T(128)} %param.16) | copy-start | bytes 1540
Sparse Core Ops, SparseCore 0:
  8.9 23.6 all-gather.1
where the time goes:
time: 205 us; the launch traced here: 204 us
  other arithmetic  82.1 us (40%)
  waiting for transfers between devices  34.9 us (17%)
  matrix products  28.9 us (14%)
  blocking collectives  25.5 us (12%)
  starting transfers between devices  15.5 us (8%)
  between operations  13.7 us (7%)
  local copies, waits for them, and re-layouts  2.82 us (1%)
    another operation x3, other arithmetic, block_parts(): jax.scipy.linalg.solve_triangular(lower, stacked, lower=True, unit_diagon...  78.7 us
    ppermute x7, waiting for transfers between devices, passed_along(): lax.ppermute(value, axis, [(source, source + steps) for source in range(l...  34.1 us
    dot_general x59, matrix products, matmul(): jnp.dot(left, right, precision=lax.Precision.HIGHEST, preferred_element_t...  25.6 us
    all_to_all x1, blocking collectives, shards(): lax.all_to_all(full_rows, 'head', split_axis=1, concat_axis=0, tiled=True)  16.9 us
    ppermute x7, starting transfers between devices, passed_along(): lax.ppermute(value, axis, [(source, source + steps) for source in range(l...  15.5 us
    all_to_all x1, blocking collectives, shards(): lax.all_to_all(normed, 'head', split_axis=0, concat_axis=1, tiled=True)  8.6 us
  transfers between devices with their start and end apart: 8, of which 7 were waited for; matrix products, arithmetic and copies ran while one was open for 54% of the time, Pallas kernels for 0%

commit v1 on v0

--- a/solution.py
+++ b/solution.py
@@ -5,6 +5,12 @@
 
 HEAD_DIM = 128
 GROUP = 128
+
+
+def trade_parts(value, axis, split, join):
+    cells = jnp.split(value, lax.axis_size(axis), axis=split)
+    incoming = lax.all_to_all(jnp.stack(cells), axis, 0, 0)
+    return jnp.concatenate(incoming, axis=join)
 
 
 def passed_along(value, axis, steps):
@@ -87,7 +93,7 @@
         lax.all_gather(w_out, "head", axis=1, tiled=True),
         preferred_element_type=jnp.float32,
     ).astype(jnp.bfloat16)
-    return lax.all_to_all(full_rows, "head", split_axis=1, concat_axis=0, tiled=True)
+    return trade_parts(full_rows, "head", 1, 0)
 
 
 def solution(mesh):

time: 205 us -> 205 us (level)
  no operation moved by 1% of the time
where the time goes in v1:
time: 205 us; the launch traced here: 204 us
  other arithmetic  82.2 us (40%)
  waiting for transfers between devices  34.9 us (17%)
  matrix products  28.9 us (14%)
  blocking collectives  25.5 us (12%)
  starting transfers between devices  15.5 us (8%)
  between operations  13.7 us (7%)
  local copies, waits for them, and re-layouts  2.84 us (1%)
    another operation x3, other arithmetic, block_parts(): jax.scipy.linalg.solve_triangular(lower, stacked, lower=True, unit_diagon...  78.7 us
    ppermute x7, waiting for transfers between devices, passed_along(): lax.ppermute(value, axis, [(source, source + steps) for source in range(l...  34.1 us
    dot_general x59, matrix products, matmul(): jnp.dot(left, right, precision=lax.Precision.HIGHEST, preferred_element_t...  25.6 us
    all_to_all x1, blocking collectives, trade_parts(): incoming = lax.all_to_all(jnp.stack(cells), axis, 0, 0)  16.9 us
    ppermute x7, starting transfers between devices, passed_along(): lax.ppermute(value, axis, [(source, source + steps) for source in range(l...  15.5 us
    all_to_all x1, blocking collectives, shards(): lax.all_to_all(normed, 'head', split_axis=0, concat_axis=1, tiled=True)  8.61 us
  transfers between devices with their start and end apart: 8, of which 7 were waited for; matrix products, arithmetic and copies ran while one was open for 54% of the time, Pallas kernels for 0%

profile of v1, /device:TPU:24, one launch (start us, length us, event | category | flops | bytes accessed | tf_op | source)
XLA Modules:
  0.0 204.5 jit_solution(3310499764938694517)
XLA Ops:
  6.5 0.7 all-gather.2.cloned.1.call-update
  7.3 1.2 fusion.36
  8.5 1.2 convert_divide_fusion.1
  9.8 1.9 fusion.31
  11.8 78.6 %custom-call.4 = f32[8,1,128,128]{2,3,1,0:T(8,128)S(1)} custom-call(f32[8,1,128,128]{3,2,1,0:T(8,128)S(1)} %fusion.31), custom_call_target="InvertDiagBlocksLowerTriangular" | custom-call | tf_op jit(solution)/shard_map/vmap(jit(_solve_triangular))/triangular_solve | solution.py:40
  90.4 0.2 broadcast_multiply_fusion
  90.6 1.0 fusion.32
  91.6 1.0 convolution_subtract_fusion.1
  92.7 1.0 fusion.44
  93.7 1.1 fusion.47
  94.8 5.2 %while.40 = (s32[]{:T(128)}, f32[128,128]{0,1:T(8,128)S(1)}, f32[128,128]{0,1:T(8,128)S(1)}, f32[8,128,128]{2,1,0:T(8,128)S(1)}, f32[8,128,128]{1,2,0:T(8,128)S(1)}) while((s32[]{:T(128)}, f32[128,128]{0,1:T(8,128)S(1)}, f32[128,128]{0,1:T(8,128)S(1)}, f32[8,128,128]{2,1,0:T(8,128)S(1)}, ...), condition=%wide.region_2.3_spmd.clone.clone, body=%wide.region_1.0_spmd.clone.sunk.clone | while | flops 50364416 | bytes 721995 | solution.py:70
  94.8 0.3 fusion.116
  95.2 0.3 convolution_bitcast_fusion.5
  95.5 0.3 fusion.116
  95.8 0.3 convolution_bitcast_fusion.5
  96.1 0.3 fusion.116
  96.5 0.3 convolution_bitcast_fusion.5
  96.8 0.3 fusion.116
  97.1 0.3 convolution_bitcast_fusion.5
  97.4 0.3 fusion.116
  97.7 0.3 convolution_bitcast_fusion.5
  98.1 0.3 fusion.116
  98.4 0.3 convolution_bitcast_fusion.5
  98.7 0.3 fusion.116
  99.0 0.3 convolution_bitcast_fusion.5
  99.4 0.3 fusion.116
  99.7 0.3 convolution_bitcast_fusion.5
  100.2 51.2 %while.38 = (s32[]{:T(128)}, f32[128,128]{1,0:T(8,128)S(1)}, f32[128,128]{1,0:T(8,128)S(1)}, f32[128,128]{1,0:T(8,128)S(1)}) while((s32[]{:T(128)}, f32[128,128]{1,0:T(8,128)S(1)}, f32[128,128]{1,0:T(8,128)S(1)}, f32[128,128]{1,0:T(8,128)S(1)}) %tuple.75), condition=%wide.region_4.5_spmd.clone, body=%wide.region_3.4_spmd.sunk.clone | while | flops 25182208 | bytes 524381 | solution.py:77
  100.4 3.4 %collective-permute-start = (f32[128,128]{1,0:T(8,128)S(1)}, f32[128,128]{1,0:T(8,128)S(1)}, u32[]{:S(2)}, u32[]{:S(2)}) collective-permute-start(f32[128,128]{1,0:T(8,128)S(1)} %convolution_add_fusion.4), channel_id=1, source_target_pairs={{0,4},{4,8},{8,12},{12,16},{16,20},{20,24},{24,28},{1,5},{5,9},{9,... | collective-permute-start | bytes 196616 | tf_op jit(solution)/shard_map/while/body/eval_jaxpr/ppermute | solution.py:19
  103.8 3.6 %collective-permute-done = f32[128,128]{1,0:T(8,128)S(1)} collective-permute-done((f32[128,128]{1,0:T(8,128)S(1)}, f32[128,128]{1,0:T(8,128)S(1)}, u32[]{:S(2)}, u32[]{:S(2)}) %collective-permute-start) | collective-permute-done | bytes 65568 | tf_op jit(solution)/shard_map/while/body/eval_jaxpr/ppermute | solution.py:19
  107.7 2.5 %collective-permute-start = (f32[128,128]{1,0:T(8,128)S(1)}, f32[128,128]{1,0:T(8,128)S(1)}, u32[]{:S(2)}, u32[]{:S(2)}) collective-permute-start(f32[128,128]{1,0:T(8,128)S(1)} %convolution_add_fusion.4), channel_id=1, source_target_pairs={{0,4},{4,8},{8,12},{12,16},{16,20},{20,24},{24,28},{1,5},{5,9},{9,... | collective-permute-start | bytes 196616 | tf_op jit(solution)/shard_map/while/body/eval_jaxpr/ppermute | solution.py:19
  110.2 4.5 %collective-permute-done = f32[128,128]{1,0:T(8,128)S(1)} collective-permute-done((f32[128,128]{1,0:T(8,128)S(1)}, f32[128,128]{1,0:T(8,128)S(1)}, u32[]{:S(2)}, u32[]{:S(2)}) %collective-permute-start) | collective-permute-done | bytes 65568 | tf_op jit(solution)/shard_map/while/body/eval_jaxpr/ppermute | solution.py:19
  115.0 1.9 collective-permute-start
  116.9 5.1 %collective-permute-done = f32[128,128]{1,0:T(8,128)S(1)} collective-permute-done((f32[128,128]{1,0:T(8,128)S(1)}, f32[128,128]{1,0:T(8,128)S(1)}, u32[]{:S(2)}, u32[]{:S(2)}) %collective-permute-start) | collective-permute-done | bytes 65568 | tf_op jit(solution)/shard_map/while/body/eval_jaxpr/ppermute | solution.py:19
  122.2 1.9 collective-permute-start
  124.2 5.1 %collective-permute-done = f32[128,128]{1,0:T(8,128)S(1)} collective-permute-done((f32[128,128]{1,0:T(8,128)S(1)}, f32[128,128]{1,0:T(8,128)S(1)}, u32[]{:S(2)}, u32[]{:S(2)}) %collective-permute-start) | collective-permute-done | bytes 65568 | tf_op jit(solution)/shard_map/while/body/eval_jaxpr/ppermute | solution.py:19
  129.5 1.9 collective-permute-start
  131.4 5.4 %collective-permute-done = f32[128,128]{1,0:T(8,128)S(1)} collective-permute-done((f32[128,128]{1,0:T(8,128)S(1)}, f32[128,128]{1,0:T(8,128)S(1)}, u32[]{:S(2)}, u32[]{:S(2)}) %collective-permute-start) | collective-permute-done | bytes 65568 | tf_op jit(solution)/shard_map/while/body/eval_jaxpr/ppermute | solution.py:19
  137.1 1.9 collective-permute-start
  139.0 5.1 %collective-permute-done = f32[128,128]{1,0:T(8,128)S(1)} collective-permute-done((f32[128,128]{1,0:T(8,128)S(1)}, f32[128,128]{1,0:T(8,128)S(1)}, u32[]{:S(2)}, u32[]{:S(2)}) %collective-permute-start) | collective-permute-done | bytes 65568 | tf_op jit(solution)/shard_map/while/body/eval_jaxpr/ppermute | solution.py:19
  144.4 1.9 collective-permute-start
  146.3 5.1 %collective-permute-done = f32[128,128]{1,0:T(8,128)S(1)} collective-permute-done((f32[128,128]{1,0:T(8,128)S(1)}, f32[128,128]{1,0:T(8,128)S(1)}, u32[]{:S(2)}, u32[]{:S(2)}) %collective-permute-start) | collective-permute-done | bytes 65568 | tf_op jit(solution)/shard_map/while/body/eval_jaxpr/ppermute | solution.py:19
  152.0 1.2 convolution_select_fusion
  153.2 14.8 %while.39 = (s32[]{:T(128)}, f32[128,128]{0,1:T(8,128)S(1)}, f32[8,128,128]{2,1,0:T(8,128)S(1)}, f32[8,128,128]{2,1,0:T(8,128)S(1)}, f32[8,128,128]{1,2,0:T(8,12...) while((s32[]{:T(128)}, f32[128,128]{0,1:T(8,128)S(1)}, ...), condition=%wide.region_7.8_spmd.clone, body=%wide.region_6.7_spmd.sunk.clone | while | flops 100712448 | bytes 1117281 | solution.py:83
  153.2 1.1 convolution_subtract_fusion.4
  154.7 0.3 fusion.109
  155.1 1.1 convolution_subtract_fusion.4
  156.6 0.3 fusion.109
  156.9 1.1 convolution_subtract_fusion.4
  158.4 0.3 fusion.109
  158.8 1.1 convolution_subtract_fusion.4
  160.3 0.3 fusion.109
  160.6 1.1 convolution_subtract_fusion.4
  162.1 0.3 fusion.109
  162.5 1.1 convolution_subtract_fusion.4
  164.0 0.3 fusion.109
  164.3 1.1 convolution_subtract_fusion.4
  165.8 0.3 fusion.109
  166.2 1.1 convolution_subtract_fusion.4
  167.7 0.3 fusion.109
  168.4 8.6 %all_to_all.21 = bf16[4,256,128]{2,1,0:T(8,128)(2,1)S(1)} all-to-all(bf16[4,256,128]{2,1,0:T(8,128)(2,1)S(1)} %fusion.39), channel_id=1, replica_groups=mesh['ctx'=8,'head'=4] {'head'}, dimensions={0} | all-to-all | bytes 524288 | tf_op jit(solution)/shard_map/all_to_all | solution.py:90
  177.2 2.3 %convolution_convert_fusion = bf16[256,2048]{1,0:T(8,128)(2,1)S(1)} fusion(bf16[256,512]{0,1:T(8,128)(2,1)S(1)} %bitcast.150, bf16[512,2048]{1,0:T(8,128)(2,1)} %all-gather.2.cloned.1.call-done), kind=kOutput, calls=%fused_computation.33 | convolution fusion | flops 537395200 | bytes 3407872 | tf_op jit(solution)/shard_map/dot_general | solution.py:91
  179.8 16.9 %all_to_all.22 = bf16[4,256,512]{2,1,0:T(8,128)(2,1)S(1)} all-to-all(bf16[4,256,512]{2,1,0:T(8,128)(2,1)S(1)} %pad_maximum_fusion), channel_id=1, replica_groups=mesh['ctx'=8,'head'=4] {'head'}, dimensions={0} | all-to-all | bytes 2097152 | tf_op jit(solution)/shard_map/all_to_all | solution.py:12
  196.7 1.0 copy.73
  (79 shorter events, 6.6 us)
Async XLA Ops:
  6.5 83.8 %copy-start.2 = (f32[1,1024]{1,0:T(1,128)S(1)}, f32[1,1024]{1,0:T(1,128)}, u32[]{:S(2)}) copy-start(f32[1,1024]{1,0:T(1,128)} %param.15) | copy-start | bytes 12292
  6.5 83.8 %copy-start.1 = (bf16[1024,128]{1,0:T(8,128)(2,1)S(1)}, bf16[1024,128]{1,0:T(8,128)(2,1)}, u32[]{:S(2)}) copy-start(bf16[1024,128]{1,0:T(8,128)(2,1)} %param.14) | copy-start | bytes 786436
  6.5 170.7 %all-gather.2.cloned.1.call-start = ((), (), s32[]{:S(2)}) async-start(), calls=%async_computation.2 | async-start | bytes 2621440 | tf_op jit(solution)/shard_map/all_gather | solution.py:93
  94.8 56.7 %copy-start = (bf16[1024,128]{1,0:T(8,128)(2,1)S(1)}, bf16[1024,128]{1,0:T(8,128)(2,1)}, u32[]{:S(2)}) copy-start(bf16[1024,128]{1,0:T(8,128)(2,1)} %param.12) | copy-start | bytes 786436
  100.4 7.1 %collective-permute-start = (f32[128,128]{1,0:T(8,128)S(1)}, f32[128,128]{1,0:T(8,128)S(1)}, u32[]{:S(2)}, u32[]{:S(2)}) collective-permute-start(f32[128,128]{1,0:T(8,128)S(1)} %convolution_add_fusion.4), channel_id=1, source_target_pairs={{0,4},{4,8},{8,12},{12,16},{16,20},{20,24},{24,28},{1,5},{5,9},{9,... | collective-permute-start | bytes 196616 | tf_op jit(solution)/shard_map/while/body/eval_jaxpr/ppermute | solution.py:19
  107.7 7.1 %collective-permute-start = (f32[128,128]{1,0:T(8,128)S(1)}, f32[128,128]{1,0:T(8,128)S(1)}, u32[]{:S(2)}, u32[]{:S(2)}) collective-permute-start(f32[128,128]{1,0:T(8,128)S(1)} %convolution_add_fusion.4), channel_id=1, source_target_pairs={{0,4},{4,8},{8,12},{12,16},{16,20},{20,24},{24,28},{1,5},{5,9},{9,... | collective-permute-start | bytes 196616 | tf_op jit(solution)/shard_map/while/body/eval_jaxpr/ppermute | solution.py:19
  115.0 7.1 %collective-permute-start = (f32[128,128]{1,0:T(8,128)S(1)}, f32[128,128]{1,0:T(8,128)S(1)}, u32[]{:S(2)}, u32[]{:S(2)}) collective-permute-start(f32[128,128]{1,0:T(8,128)S(1)} %convolution_add_fusion.4), channel_id=1, source_target_pairs={{0,4},{4,8},{8,12},{12,16},{16,20},{20,24},{24,28},{1,5},{5,9},{9,... | collective-permute-start | bytes 196616 | tf_op jit(solution)/shard_map/while/body/eval_jaxpr/ppermute | solution.py:19
  122.2 7.1 %collective-permute-start = (f32[128,128]{1,0:T(8,128)S(1)}, f32[128,128]{1,0:T(8,128)S(1)}, u32[]{:S(2)}, u32[]{:S(2)}) collective-permute-start(f32[128,128]{1,0:T(8,128)S(1)} %convolution_add_fusion.4), channel_id=1, source_target_pairs={{0,4},{4,8},{8,12},{12,16},{16,20},{20,24},{24,28},{1,5},{5,9},{9,... | collective-permute-start | bytes 196616 | tf_op jit(solution)/shard_map/while/body/eval_jaxpr/ppermute | solution.py:19
  129.5 7.4 %collective-permute-start = (f32[128,128]{1,0:T(8,128)S(1)}, f32[128,128]{1,0:T(8,128)S(1)}, u32[]{:S(2)}, u32[]{:S(2)}) collective-permute-start(f32[128,128]{1,0:T(8,128)S(1)} %convolution_add_fusion.4), channel_id=1, source_target_pairs={{0,4},{4,8},{8,12},{12,16},{16,20},{20,24},{24,28},{1,5},{5,9},{9,... | collective-permute-start | bytes 196616 | tf_op jit(solution)/shard_map/while/body/eval_jaxpr/ppermute | solution.py:19
  137.1 7.1 %collective-permute-start = (f32[128,128]{1,0:T(8,128)S(1)}, f32[128,128]{1,0:T(8,128)S(1)}, u32[]{:S(2)}, u32[]{:S(2)}) collective-permute-start(f32[128,128]{1,0:T(8,128)S(1)} %convolution_add_fusion.4), channel_id=1, source_target_pairs={{0,4},{4,8},{8,12},{12,16},{16,20},{20,24},{24,28},{1,5},{5,9},{9,... | collective-permute-start | bytes 196616 | tf_op jit(solution)/shard_map/while/body/eval_jaxpr/ppermute | solution.py:19
  144.4 7.1 %collective-permute-start = (f32[128,128]{1,0:T(8,128)S(1)}, f32[128,128]{1,0:T(8,128)S(1)}, u32[]{:S(2)}, u32[]{:S(2)}) collective-permute-start(f32[128,128]{1,0:T(8,128)S(1)} %convolution_add_fusion.4), channel_id=1, source_target_pairs={{0,4},{4,8},{8,12},{12,16},{16,20},{20,24},{24,28},{1,5},{5,9},{9,... | collective-permute-start | bytes 196616 | tf_op jit(solution)/shard_map/while/body/eval_jaxpr/ppermute | solution.py:19
  153.2 15.0 %copy-start.3 = (f32[128]{0:T(128)S(1)}, f32[128]{0:T(128)}, u32[]{:S(2)}) copy-start(f32[128]{0:T(128)} %param.16) | copy-start | bytes 1540
Sparse Core Ops, SparseCore 0:
  8.9 23.6 all-gather.1
